TPU v7x, 32 devices: a whole 2x2x4 slice. The times are simulated.
32 devices in a mesh: grp: 4 (over x, core), wide: 8 (over z, y).
Axes of the slice: x: 2, y: 2, z: 4, core: 2. Of those that a mesh axis runs over, the one named last changes fastest.
Arguments:
- expression: float32 [1024, 4096], P(('grp', 'wide'))
- assignment: int32 [16], replicated, may hold values from 0 to 15, each once
- pairing: int32 [2, 16], replicated, may hold values from 0 to 15, as said below
Outputs:
- cross_scores: float32 [2, 16, 256, 256], P(None, 'wide', 'grp')
Inputs may be any that keep to these rules, and one draw needn't show every extreme that they name: Row r of pairing is round r of one round-robin plan over the 16 panels: every panel has a partner other than itself, and the partner's partner is the panel.
All inputs are finite; a program needn't handle non-finite values.
Results may differ from a plain program's by a relative error of at most 0.0043.
Values may be sent and summed in bfloat16 or wider, within the bound.
No kernel may reach another device: no remote copies, remote signals or barrier semaphores. Data moves between devices by JAX's collectives and lax.ppermute only.
A program may use at most 192 MiB of HBM per device.

v0:
```python
import jax
import jax.numpy as jnp
from jax import lax
from jax.sharding import PartitionSpec as P

PANEL = 256


def cross_terms(received):
    count = received.shape[1]
    cells = received.shape[2]
    width = received.shape[3]
    blocks = received.reshape(count, cells, width // received_panel_width(), received_panel_width())
    own = blocks[:, :, 0]
    partners = blocks[:, :, 1:]
    return jnp.einsum("mca,mcrb->rmab", own, partners, preferred_element_type=jnp.float32)


def received_panel_width():
    return PANEL


def shards(expression, assignment, pairing):
    n_wide = lax.axis_size("wide")
    n_grp = lax.axis_size("grp")
    cells = expression.shape[0]
    pan_dev = assignment.shape[0] // n_wide
    panel = expression.shape[1] // assignment.shape[0]
    rounds = pairing.shape[0]
    total = cells * n_wide * n_grp
    own_ids = assignment.reshape(n_wide, pan_dev, 1)
    partner_ids = pairing[:, assignment].T.reshape(n_wide, pan_dev, rounds)
    panel_ids = jnp.concatenate([own_ids, partner_ids], axis=2)
    columns = (panel_ids[..., None] * panel + jnp.arange(panel, dtype=jnp.int32)).reshape(-1)
    span = (1 + rounds) * panel
    picked = (
        jnp.take(expression, columns, axis=1)
        .reshape(cells, n_wide, pan_dev, span)
        .transpose(1, 2, 0, 3)
    )
    received = lax.all_to_all(picked, "wide", split_axis=0, concat_axis=2, tiled=True)
    sums = lax.psum(
        (
            jnp.sum(received, axis=2, keepdims=True),
            jnp.sum(received * received, axis=2, keepdims=True),
        ),
        "grp",
    )
    mean = sums[0] / total
    var = sums[1] / total - mean * mean
    scaled = ((received - mean) * lax.rsqrt(var + 1e-05)).astype(jnp.bfloat16)
    partial_tiles = cross_terms(scaled)
    rows_dev = panel // n_grp
    summed = lax.psum(partial_tiles, "grp")
    mine = lax.dynamic_slice_in_dim(summed, lax.axis_index("grp") * rows_dev, rows_dev, 2)
    return mine * total ** (-0.5)


def solution(mesh):
    placed = (P(("grp", "wide"), None), P(), P())
    return jax.shard_map(
        shards, mesh=mesh, in_specs=placed, out_specs=P(None, "wide", "grp", None), check_vma=False
    )
```

profile of v0, /device:TPU:0, one launch (start us, length us, event | category | flops | bytes accessed | tf_op | source)
XLA Modules:
  0.0 160.9 jit_solution(13995582573003539010)
XLA Ops:
  6.5 0.0 all-reduce.3.cloned.1.call-start
  6.5 0.7 compare_select_fusion.2
  7.2 0.7 concatenate.11
  7.9 0.1 copy.34
  8.0 0.8 copy.32
  8.8 0.6 gather_fusion
  9.3 0.1 copy.35
  9.4 0.1 copy.36
  9.5 0.1 iota_add_fusion
  9.6 0.1 add.77
  9.7 0.1 reshape.107
  9.8 0.1 compare_select_fusion
  9.9 1.6 %copy.39 = f32[32,4096]{0,1:T(8,128)S(1)} copy(f32[32,4096]{1,0:T(8,128)} %param.3) | data formatting | bytes 1048576 | tf_op args[0]
  11.6 41.0 %gather_fusion.1 = f32[12288,32]{1,0:T(8,128)} fusion(f32[32,4096]{0,1:T(8,128)S(1)} %copy.39, s32[12288]{0:T(1024)S(1)} %broadcast_clamp_fusion), kind=kCustom, calls=%fused_computation.1 | custom fusion | bytes 3194880 | tf_op jit(solution)/shard_map/jit(_take)/gather | solution.py:37
  52.6 4.4 %copy.40 = f32[32,8,2,768]{3,0,2,1:T(8,128)S(1)} copy(f32[32,8,2,768]{0,3,2,1:T(8,128)} %bitcast.26) | data formatting | bytes 3145728 | tf_op jit(solution)/shard_map/jit(_take)/gather | solution.py:37
  56.9 0.2 select_bitcast_fusion
  57.1 44.1 %all_to_all.18 = f32[8,2,32,768]{3,2,1,0:T(8,128)S(1)} all-to-all(f32[8,2,32,768]{3,2,1,0:T(8,128)S(1)} %select_bitcast_fusion), channel_id=1, replica_groups=mesh['grp'=4,'wide'=8] {'wide'}, dimensions={0} | all-to-all | bytes 3145728 | tf_op jit(solution)/shard_map/all_to_all | solution.py:41
  101.2 0.1 copy.41
  101.4 1.9 %all_to_all.16 = f32[2,256,3,256]{3,2,1,0:T(4,128)} reshape(f32[1,2,8,32,768]{4,3,2,1,0:T(8,128)S(1)} %copy.41) | data formatting | bytes 3145728 | tf_op jit(solution)/shard_map/all_to_all | solution.py:41
  103.3 0.2 bitcast_reduce_fusion
  103.4 10.1 %all-reduce = (f32[1,2,1,768]{3,1,2,0:T(2,128)S(1)}, f32[1,2,1,768]{3,1,2,0:T(2,128)S(1)}) all-reduce(f32[1,2,1,768]{3,1,2,0:T(2,128)S(1)} %bitcast.29, f32[1,2,1,768]{3,1,2,0:T(2,128)S(1)} %bitcast.28), channel_id=1, replica_groups=mesh['grp'=4,'wide'=8] {'grp'}, use_global_device_ids=true, to_apply=%region_3.4 | all-reduce | flops 3072 | bytes 24576 | tf_op jit(solution)/shard_map/psum | solution.py:42
  113.6 1.9 %fusion.1 = bf16[2,256,3,256]{3,1,0,2:T(8,128)(2,1)S(1)} fusion(f32[2,256,3,256]{3,2,1,0:T(4,128)} %all_to_all.16, f32[2,3,256]{2,0,1:T(2,128)S(1)} %bitcast.31, f32[2,3,256]{2,0,1:T(2,128)S(1)} %bitcast.30), kind=kLoop, calls=%fused_computation.4 | loop fusion | flops 1179648 | bytes 2371584 | tf_op jit(solution)/shard_map/convert_element_type | solution.py:51
  115.5 1.4 convolution_bitcast_fusion
  116.9 0.0 all-reduce.3.cloned.1.call-update
  116.9 35.5 %all-reduce.3.cloned.1.call-done = f32[2,2,256,256]{3,2,1,0:T(8,128)} async-done(((f32[2,2,256,256]{3,2,1,0:T(8,128)}), f32[2,2,256,256]{3,2,1,0:T(8,128)}) %all-reduce.3.cloned.1.call-update) | async-done | bytes 1048592 | tf_op jit(solution)/shard_map/psum | solution.py:54
  152.4 1.7 %dynamic-slice_multiply_fusion = f32[2,2,64,256]{3,2,1,0:T(8,128)} fusion(f32[2,2,256,256]{3,2,1,0:T(8,128)} %all-reduce.3.cloned.1.call-done, s32[]{:T(128)S(6)} %select_n.32), kind=kLoop, calls=%fused_computation.10 | loop fusion | flops 65536 | bytes 524292 | tf_op jit(solution)/shard_map/mul | solution.py:56
  (6 shorter events, 0.1 us)
Async XLA Ops:
  6.5 145.9 %all-reduce.3.cloned.1.call-start = ((), (), s32[]{:S(2)}) async-start(), calls=%async_computation.1 | async-start | bytes 2097152 | tf_op jit(solution)/shard_map/psum | solution.py:54
Sparse Core Ops, SparseCore 0:
  117.0 35.3 all-reduce.2
where the time goes:
time: 161 us
  blocking collectives  54.2 us (34%)
  local copies, waits for them, and re-layouts  51.5 us (32%)
  waiting for transfers between devices  35.5 us (22%)
  between operations  13.5 us (8%)
  other arithmetic  4.75 us (3%)
    gather x2, local copies, waits for them, and re-layouts, shards(): jnp.take(expression, columns, axis=1).reshape(cells, n_wide, pan_dev, span)  45.4 us
    all_to_all x1, blocking collectives, shards(): lax.all_to_all(picked, 'wide', split_axis=0, concat_axis=2, tiled=True)  44.1 us
    psum x1, waiting for transfers between devices, shards(): summed = lax.psum(partial_tiles, 'grp')  35.5 us
    psum x1, blocking collectives, shards(): lax.psum((jnp.sum(received, axis=2, keepdims=True), jnp.sum(received * re...  10.1 us
  transfers between devices with their start and end apart: 1, of which 1 were waited for; matrix products, arithmetic and copies ran while one was open for 0% of the time, Pallas kernels for 0%

commit v1 on v0

v1 whole, which is shorter than its diff:
```python
import functools

import jax
import jax.numpy as jnp
from jax import lax
from jax.experimental import pallas as pl
from jax.experimental.pallas import tpu as pltpu
from jax.sharding import PartitionSpec as P

SLOTS = 2
ROUNDS = 2
PICKED = SLOTS * (1 + ROUNDS)
SIDE = 16
F32 = jnp.float32
BF16 = jnp.bfloat16


def split_two(value):
    high = value.astype(BF16).astype(F32)
    return high, value - high


def prep_kernel(assignment, pairing, x_ref, out_ref, centred, high_rows, low_rows, side):
    cells, genes = x_ref.shape
    panels = assignment.shape[0]
    panel = genes // panels
    n_wide = out_ref.shape[0]

    def one_panel(p, carry):
        start = pl.multiple_of(p * panel, panel)
        block = x_ref[:, pl.ds(start, panel)]
        mean = jnp.sum(block, axis=0, keepdims=True) * (1.0 / cells)
        high, rest = split_two(mean)
        low = rest.astype(BF16).astype(F32)
        centred[p] = (block - (high + low)).astype(BF16)
        high_rows[pl.ds(p, 1), :] = high
        low_rows[pl.ds(p, 1), :] = low
        return carry

    lax.fori_loop(0, panels, one_panel, 0, unroll=panels <= 16)
    side[...] = jnp.zeros_like(side)

    def one_message(w, carry):
        for s in range(SLOTS):
            own = assignment[w * SLOTS + s]
            for k in range(1 + ROUNDS):
                p = own if k == 0 else pairing[k - 1, own]
                j = s if k == 0 else SLOTS + s * ROUNDS + k - 1
                out_ref[w, pl.ds(j * cells, cells), :] = centred[p]
                side[pl.ds(j, 1), :] = high_rows[pl.ds(p, 1), :]
                side[pl.ds(PICKED + j, 1), :] = low_rows[pl.ds(p, 1), :]
        out_ref[w, pl.ds(PICKED * cells, SIDE), :] = side[...].astype(BF16)
        return carry

    lax.fori_loop(0, n_wide, one_message, 0, unroll=n_wide <= 8)


def gram_kernel(cells, panel, place, here_ref, there_ref, near_ref, far_ref, stat_ref, tile):
    n_wide = here_ref.shape[0]
    blocks = 2 * n_wide
    rows = blocks * cells
    quarter = panel // 4

    def part(start, size):
        halves = [r[:, pl.ds(start, size), :].reshape(n_wide * size, panel) for r in (here_ref, there_ref)]
        return jnp.concatenate(halves, axis=0)

    member = lax.broadcasted_iota(jnp.int32, (blocks, rows), 1) // cells
    member = (member == lax.broadcasted_iota(jnp.int32, (blocks, rows), 0)).astype(BF16)
    side = jnp.concatenate(
        [r[:, pl.ds(PICKED * cells, SIDE), :].astype(F32) for r in (here_ref, there_ref)], axis=0
    )
    left, right, means, squares = [], [], [], []
    for j in range(PICKED):
        data = part(j * cells, cells)
        sums = jnp.dot(member, data, preferred_element_type=F32)
        block_mean = side[:, j, :] + side[:, PICKED + j, :] + sums * (1.0 / cells)
        mean = jnp.sum(block_mean, axis=0, keepdims=True) * (1.0 / blocks)
        shift = block_mean - mean
        wide_data = data.astype(F32)
        square = jnp.sum(wide_data * wide_data, axis=0, keepdims=True) + jnp.sum(
            cells * (shift * shift) - sums * sums * (1.0 / cells), axis=0, keepdims=True
        )
        means.append(mean)
        squares.append(square)
        high, low = split_two(shift)
        scale = cells // 8
        if j < SLOTS:
            extra = [8.0 * high, 8.0 * low, 8.0 * high, sums * 0.125]
        else:
            extra = [scale * high, scale * high, scale * low, sums * (-8.0 / cells)]
        (left if j < SLOTS else right).append(
            jnp.concatenate([data, jnp.concatenate(extra, axis=0).astype(BF16)], axis=0)
        )
    stats = jnp.concatenate(means + squares + [jnp.zeros((SIDE - 2 * PICKED, panel), F32)], axis=0)
    stat_ref[...] = stats
    mine = place[0]
    near = pl.multiple_of(mine * quarter, quarter)
    far = pl.multiple_of(((mine + 2) % 4) * quarter, quarter)
    for s in range(SLOTS):
        for r in range(ROUNDS):
            t = s * ROUNDS + r
            tile[...] = lax.dot_general(
                left[s], right[t], (((0,), (0,)), ((), ())), preferred_element_type=F32
            )
            near_ref[pl.ds(t * quarter, quarter), :] = tile[pl.ds(near, quarter), :]
            far_ref[pl.ds(t * quarter, quarter), :] = tile[pl.ds(far, quarter), :].astype(BF16)
    high, rest = split_two(stats)
    middle, low = split_two(rest)
    base = SLOTS * ROUNDS * quarter
    for i, value in enumerate((high, middle, low)):
        far_ref[pl.ds(base + i * SIDE, SIDE), :] = value.astype(BF16)


def finish_kernel(total, panel, place, near_ref, far_ref, stat_ref, out_ref, columns):
    quarter = panel // 4
    base = SLOTS * ROUNDS * quarter
    other = sum(far_ref[pl.ds(base + i * SIDE, SIDE), :].astype(F32) for i in (2, 1, 0))
    stats = stat_ref[...]
    both = stats + other
    gap = (stats - other)[0:8]
    var = (both[PICKED : PICKED + 8] * (1.0 / total)) + (gap * gap) * 0.25
    inv = lax.rsqrt(var + 1e-05)
    columns[...] = jnp.concatenate([gap, inv], axis=0).T
    mine = pl.multiple_of(place[0] * quarter, quarter)
    side = columns[pl.ds(mine, quarter), :]
    for s in range(SLOTS):
        gap_row = side[:, s : s + 1]
        inv_row = side[:, 8 + s : 9 + s] * total ** (-0.5)
        for r in range(ROUNDS):
            t = s * ROUNDS + r
            j = SLOTS + t
            rows = pl.ds(t * quarter, quarter)
            tile = near_ref[rows, :] + far_ref[rows, :].astype(F32)
            tile = tile + gap_row * (gap[j : j + 1] * (total / 4))
            out_ref[r, s] = tile * inv_row * inv[j : j + 1]


def shards(expression, assignment, pairing):
    n_wide = lax.axis_size("wide")
    n_grp = lax.axis_size("grp")
    cells, genes = expression.shape
    panel = genes // assignment.shape[0]
    panels = assignment.shape[0]
    quarter = panel // n_grp
    total = cells * n_wide * n_grp
    place = lax.axis_index("grp").reshape(1).astype(jnp.int32)
    smem = pl.BlockSpec(memory_space=pltpu.SMEM)
    vmem = pl.BlockSpec(memory_space=pltpu.VMEM)
    message = PICKED * cells + SIDE
    sent = pl.pallas_call(
        prep_kernel,
        out_shape=jax.ShapeDtypeStruct((n_wide, message, panel), BF16),
        in_specs=[smem, smem, vmem],
        out_specs=vmem,
        scratch_shapes=[
            pltpu.VMEM((panels, cells, panel), BF16),
            pltpu.VMEM((panels, panel), F32),
            pltpu.VMEM((panels, panel), F32),
            pltpu.VMEM((SIDE, panel), F32),
        ],
        name="prep",
    )(assignment, pairing, expression)
    here = lax.all_to_all(sent, "wide", split_axis=0, concat_axis=0, tiled=True)
    there = lax.ppermute(here, "grp", [(i, i ^ 1) for i in range(n_grp)])
    tiles = SLOTS * ROUNDS * quarter
    near, far, stats = pl.pallas_call(
        functools.partial(gram_kernel, cells, panel),
        out_shape=(
            jax.ShapeDtypeStruct((tiles, panel), F32),
            jax.ShapeDtypeStruct((tiles + 3 * SIDE, panel), BF16),
            jax.ShapeDtypeStruct((SIDE, panel), F32),
        ),
        in_specs=[smem, vmem, vmem],
        out_specs=(vmem, vmem, vmem),
        scratch_shapes=[pltpu.VMEM((panel, panel), F32)],
        compiler_params=pltpu.CompilerParams(vmem_limit_bytes=60 << 20),
        name="gram",
    )(place, here, there)
    far = lax.ppermute(far, "grp", [(i, i ^ 2) for i in range(n_grp)])
    return pl.pallas_call(
        functools.partial(finish_kernel, total, panel),
        out_shape=jax.ShapeDtypeStruct((ROUNDS, SLOTS, quarter, panel), F32),
        in_specs=[smem, vmem, vmem, vmem],
        out_specs=vmem,
        scratch_shapes=[pltpu.VMEM((panel, 16), F32)],
        name="finish",
    )(place, near, far, stats)


def solution(mesh):
    placed = (P(("grp", "wide"), None), P(), P())
    return jax.shard_map(
        shards, mesh=mesh, in_specs=placed, out_specs=P(None, "wide", "grp", None), check_vma=False
    )
```

time: 161 us -> 47.2 us (0.29)
  local copies, waits for them, and re-layouts: 51.5 us -> 1.59 us
  waiting for transfers between devices: 35.5 us -> 7.16 us
  blocking collectives: 54.2 us -> 29.4 us
  between operations: 13.5 us -> 0.01 us
  Pallas kernels: 0 us -> 7.27 us
  other arithmetic: 4.75 us -> 0 us
    gather x3 -> x0, local copies, waits for them, and re-layouts: 45.9 us -> none  [the longest x2 45.4 us: shards(): jnp.take(expression, columns, axis=1).reshape(cells, n_wide, pan_dev, span)]
    psum x1 -> x0, waiting for transfers between devices: 35.5 us -> none  [shards(): summed = lax.psum(partial_tiles, 'grp')]
    all_to_all x1, blocking collectives: 44.1 us -> 29.4 us  [shards(): here = lax.all_to_all(sent, 'wide', split_axis=0, concat_axis=0, tiled=True)]
    psum x1 -> x0, blocking collectives: 10.1 us -> none  [shards(): lax.psum((jnp.sum(received, axis=2, keepdims=True), jnp.sum(received * re...]
    pallas_call x0 -> x3, Pallas kernels: none -> 7.27 us  [the longest x1 3.08 us: shards(): pl.pallas_call(functools.partial(gram_kernel, cells, panel), out_shape=(j...]
    ppermute x0 -> x2, waiting for transfers between devices: none -> 7.16 us  [the longest x1 4.79 us: shards(): far = lax.ppermute(far, 'grp', [(i, i ^ 2) for i in range(n_grp)])]
    all_to_all x2 -> x0, local copies, waits for them, and re-layouts: 2.04 us -> none  [shards(): lax.all_to_all(picked, 'wide', split_axis=0, concat_axis=2, tiled=True)]
    convert_element_type x1 -> x0, other arithmetic: 1.88 us -> none  [shards(): scaled = ((received - mean) * lax.rsqrt(var + 1e-05)).astype(jnp.bfloat16)]
  transfers between devices with their start and end apart: 1 -> 2, of which waited for: 1 -> 2; matrix products, arithmetic and copies ran while one was open for 0% -> 0% of each run, Pallas kernels for 0% -> 0%
where the time goes in v1:
time: 47.2 us; the launch traced here: 47 us
  blocking collectives  29.4 us (62%)
  Pallas kernels  7.27 us (15%)
  waiting for transfers between devices  7.16 us (15%)
  local copies, waits for them, and re-layouts  1.59 us (3%)
  starting transfers between devices  1.5 us (3%)
    all_to_all x1, blocking collectives, shards(): here = lax.all_to_all(sent, 'wide', split_axis=0, concat_axis=0, tiled=True)  29.4 us
    ppermute x1, waiting for transfers between devices, shards(): far = lax.ppermute(far, 'grp', [(i, i ^ 2) for i in range(n_grp)])  4.79 us
    pallas_call x1, Pallas kernels, shards(): pl.pallas_call(functools.partial(gram_kernel, cells, panel), out_shape=(j...  3.08 us
    ppermute x1, waiting for transfers between devices, shards(): there = lax.ppermute(here, 'grp', [(i, i ^ 1) for i in range(n_grp)])  2.38 us
    pallas_call x1, Pallas kernels, shards(): pl.pallas_call(prep_kernel, out_shape=jax.ShapeDtypeStruct((n_wide, messa...  2.23 us
    pallas_call x1, Pallas kernels, shards(): pl.pallas_call(functools.partial(finish_kernel, total, panel), out_shape=...  1.97 us
    unnamed x6, local copies, waits for them, and re-layouts  1.59 us
    ppermute x1, starting transfers between devices, shards(): far = lax.ppermute(far, 'grp', [(i, i ^ 2) for i in range(n_grp)])  1.49 us
  transfers between devices with their start and end apart: 2, of which 2 were waited for; matrix products, arithmetic and copies ran while one was open for 0% of the time, Pallas kernels for 0%

profile of v1, /device:TPU:0, one launch (start us, length us, event | category | flops | bytes accessed | tf_op | source)
XLA Modules:
  0.0 47.0 jit_solution(2400545892757031576)
XLA Ops:
  0.0 2.2 %prep.1 = bf16[8,208,256]{2,1,0:T(8,128)(2,1)} custom-call(s32[16]{0:T(128)} %assignment.1, s32[2,16]{1,0:T(2,128)} %pairing.1, f32[32,4096]{1,0:T(8,128)} %x_ref.1), custom_call_target="tpu_custom_call" | custom-call | tf_op jit(solution)/shard_map/prep/pallas_call | solution.py:151
  2.2 29.4 %all_to_all.5.here_ref = bf16[8,208,256]{2,1,0:T(8,128)(2,1)S(1)} all-to-all(bf16[8,208,256]{2,1,0:T(8,128)(2,1)} %prep.1), channel_id=1, replica_groups=mesh['grp'=4,'wide'=8] {'wide'}, dimensions={0} | all-to-all | bytes 1703936 | tf_op jit(solution)/shard_map/all_to_all | solution.py:164
  31.7 0.0 copy-start
  31.7 0.0 collective-permute-start
  31.7 2.4 %collective-permute-done.there_ref = bf16[8,208,256]{2,1,0:T(8,128)(2,1)S(1)} collective-permute-done((bf16[8,208,256]{2,1,0:T(8,128)(2,1)S(1)}, bf16[8,208,256]{2,1,0:T(8,128)(2,1)S(1)}, u32[]{:S(2)}, u32[]{:S(2)}) %collective-permute-start) | collective-permute-done | bytes 852000 | tf_op jit(solution)/shard_map/ppermute | solution.py:165
  34.1 0.0 copy-start.1
  34.1 0.0 copy-done
  34.1 0.9 %copy-done.1 = bf16[8,208,256]{2,1,0:T(8,128)(2,1)} copy-done((bf16[8,208,256]{2,1,0:T(8,128)(2,1)}, bf16[8,208,256]{2,1,0:T(8,128)(2,1)S(1)}, u32[]{:S(2)}) %copy-start.1) | copy-done | bytes 851992
  35.0 3.1 %gram.1 = (f32[256,256]{1,0:T(8,128)}, bf16[304,256]{1,0:T(8,128)(2,1)}, f32[16,256]{1,0:T(8,128)}) custom-call(s32[1]{0:T(128)} %bitcast.place, bf16[8,208,256]{2,1,0:T(8,128)(2,1)} %copy-done, bf16[8,208,256]{2,1,0:T(8,128)(2,1)} %copy-done.1), custom_call_target="tpu_custom_call" | custom-call | tf_op jit(solution)/shard_map/gram/pallas_call | solution.py:167
  38.1 1.5 %collective-permute-start.1 = (bf16[304,256]{1,0:T(8,128)(2,1)}, bf16[304,256]{1,0:T(8,128)(2,1)S(1)}, u32[]{:S(2)}, u32[]{:S(2)}) collective-permute-start(bf16[304,256]{1,0:T(8,128)(2,1)} %get-tuple-element.9), channel_id=1, source_target_pairs={{0,16},{8,24},{16,0},{24,8},{1,17},{9,25},{17,1},{25,9},{2,18},{10... | collective-permute-start | bytes 466952 | tf_op jit(solution)/shard_map/ppermute | solution.py:180
  39.6 4.8 %collective-permute-done.1.far_ref = bf16[304,256]{1,0:T(8,128)(2,1)S(1)} collective-permute-done((bf16[304,256]{1,0:T(8,128)(2,1)}, bf16[304,256]{1,0:T(8,128)(2,1)S(1)}, u32[]{:S(2)}, u32[]{:S(2)}) %collective-permute-start.1) | collective-permute-done | bytes 155680 | tf_op jit(solution)/shard_map/ppermute | solution.py:180
  44.4 0.0 copy-start.2
  44.4 0.6 %copy-done.2 = bf16[304,256]{1,0:T(8,128)(2,1)} copy-done((bf16[304,256]{1,0:T(8,128)(2,1)}, bf16[304,256]{1,0:T(8,128)(2,1)S(1)}, u32[]{:S(2)}) %copy-start.2) | copy-done | bytes 155672
  45.0 2.0 %finish.1 = f32[2,2,64,256]{3,2,1,0:T(8,128)} custom-call(s32[1]{0:T(128)} %bitcast.place, f32[256,256]{1,0:T(8,128)} %get-tuple-element.8.near_ref, bf16[304,256]{1,0:T(8,128)(2,1)} %copy-done.2, f32[16,256]{1,0:T(8,128)} %get-tuple-element.10.stat_ref), custom_call_target="tpu_custom_call" | custom-call | tf_op jit(solution)/shard_map/finish/pallas_call | solution.py:181
Async XLA Ops:
  31.7 2.4 %copy-start = (bf16[8,208,256]{2,1,0:T(8,128)(2,1)}, bf16[8,208,256]{2,1,0:T(8,128)(2,1)S(1)}, u32[]{:S(2)}) copy-start(bf16[8,208,256]{2,1,0:T(8,128)(2,1)S(1)} %all_to_all.5.here_ref) | copy-start | bytes 2555908
  31.7 2.4 %collective-permute-start = (bf16[8,208,256]{2,1,0:T(8,128)(2,1)S(1)}, bf16[8,208,256]{2,1,0:T(8,128)(2,1)S(1)}, u32[]{:S(2)}, u32[]{:S(2)}) collective-permute-start(bf16[8,208,256]{2,1,0:T(8,128)(2,1)S(1)} %all_to_all.5.here_ref), channel_id=1, source_target_pairs={{0,8},{8,0},{16,24},{24,16},{1,9},{9,1},{17,25},{25,17},{2,10},{10... | collective-permute-start | bytes 2555912 | tf_op jit(solution)/shard_map/ppermute | solution.py:165
  34.1 0.9 %copy-start.1 = (bf16[8,208,256]{2,1,0:T(8,128)(2,1)}, bf16[8,208,256]{2,1,0:T(8,128)(2,1)S(1)}, u32[]{:S(2)}) copy-start(bf16[8,208,256]{2,1,0:T(8,128)(2,1)S(1)} %collective-permute-done.there_ref) | copy-start | bytes 2555908
  38.1 6.3 %collective-permute-start.1 = (bf16[304,256]{1,0:T(8,128)(2,1)}, bf16[304,256]{1,0:T(8,128)(2,1)S(1)}, u32[]{:S(2)}, u32[]{:S(2)}) collective-permute-start(bf16[304,256]{1,0:T(8,128)(2,1)} %get-tuple-element.9), channel_id=1, source_target_pairs={{0,16},{8,24},{16,0},{24,8},{1,17},{9,25},{17,1},{25,9},{2,18},{10... | collective-permute-start | bytes 466952 | tf_op jit(solution)/shard_map/ppermute | solution.py:180
  44.4 0.7 %copy-start.2 = (bf16[304,256]{1,0:T(8,128)(2,1)}, bf16[304,256]{1,0:T(8,128)(2,1)S(1)}, u32[]{:S(2)}) copy-start(bf16[304,256]{1,0:T(8,128)(2,1)S(1)} %collective-permute-done.1.far_ref) | copy-start | bytes 466948

commit v2 on v1

--- a/solution.py
+++ b/solution.py
@@ -136,6 +136,12 @@
             out_ref[r, s] = tile * inv_row * inv[j : j + 1]
 
 
+def on_chip(small):
+    if not small:
+        return jax.ShapeDtypeStruct, lambda value: value
+    return pltpu.VMEM, lambda value: pltpu.with_memory_space_constraint(value, pltpu.VMEM)
+
+
 def shards(expression, assignment, pairing):
     n_wide = lax.axis_size("wide")
     n_grp = lax.axis_size("grp")
@@ -148,9 +154,11 @@
     smem = pl.BlockSpec(memory_space=pltpu.SMEM)
     vmem = pl.BlockSpec(memory_space=pltpu.VMEM)
     message = PICKED * cells + SIDE
+    received_bytes = 2 * n_wide * message * panel * 2
+    array, in_vmem = on_chip(received_bytes <= 4 << 20)
     sent = pl.pallas_call(
         prep_kernel,
-        out_shape=jax.ShapeDtypeStruct((n_wide, message, panel), BF16),
+        out_shape=array((n_wide, message, panel), BF16),
         in_specs=[smem, smem, vmem],
         out_specs=vmem,
         scratch_shapes=[
@@ -167,16 +175,16 @@
     near, far, stats = pl.pallas_call(
         functools.partial(gram_kernel, cells, panel),
         out_shape=(
-            jax.ShapeDtypeStruct((tiles, panel), F32),
-            jax.ShapeDtypeStruct((tiles + 3 * SIDE, panel), BF16),
-            jax.ShapeDtypeStruct((SIDE, panel), F32),
+            array((tiles, panel), F32),
+            array((tiles + 3 * SIDE, panel), BF16),
+            array((SIDE, panel), F32),
         ),
         in_specs=[smem, vmem, vmem],
         out_specs=(vmem, vmem, vmem),
         scratch_shapes=[pltpu.VMEM((panel, panel), F32)],
-        compiler_params=pltpu.CompilerParams(vmem_limit_bytes=60 << 20),
+        compiler_params=pltpu.CompilerParams(vmem_limit_bytes=min(60 << 20, (8 << 20) + 6 * received_bytes)),
         name="gram",
-    )(place, here, there)
+    )(place, in_vmem(here), in_vmem(there))
     far = lax.ppermute(far, "grp", [(i, i ^ 2) for i in range(n_grp)])
     return pl.pallas_call(
         functools.partial(finish_kernel, total, panel),
@@ -185,7 +193,7 @@
         out_specs=vmem,
         scratch_shapes=[pltpu.VMEM((panel, 16), F32)],
         name="finish",
-    )(place, near, far, stats)
+    )(place, in_vmem(near), in_vmem(far), in_vmem(stats))
 
 
 def solution(mesh):

time: 47.2 us -> 41.1 us (0.87)
  Pallas kernels: 7.27 us -> 3.17 us
  local copies, waits for them, and re-layouts: 1.59 us -> 0 us
    pallas_call x2, Pallas kernels: 5.3 us -> 2.23 us  [the longest x1 1.33 us: shards(): pl.pallas_call(prep_kernel, out_shape=array((n_wide, message, panel), BF1...]
    unnamed x6 -> x0, local copies, waits for them, and re-layouts: 1.59 us -> none
    pallas_call x1, Pallas kernels: 1.97 us -> 0.93 us  [shards(): pl.pallas_call(functools.partial(finish_kernel, total, panel), out_shape=...]
where the time goes in v2:
time: 41.1 us; the launch traced here: 40.9 us
  blocking collectives  29.3 us (71%)
  waiting for transfers between devices  6.95 us (17%)
  Pallas kernels  3.17 us (8%)
  starting transfers between devices  1.56 us (4%)
    all_to_all x1, blocking collectives, shards(): here = lax.all_to_all(sent, 'wide', split_axis=0, concat_axis=0, tiled=True)  29.3 us
    ppermute x1, waiting for transfers between devices, shards(): far = lax.ppermute(far, 'grp', [(i, i ^ 2) for i in range(n_grp)])  4.57 us
    ppermute x1, waiting for transfers between devices, shards(): there = lax.ppermute(here, 'grp', [(i, i ^ 1) for i in range(n_grp)])  2.38 us
    ppermute x1, starting transfers between devices, shards(): far = lax.ppermute(far, 'grp', [(i, i ^ 2) for i in range(n_grp)])  1.56 us
    pallas_call x1, Pallas kernels, shards(): pl.pallas_call(prep_kernel, out_shape=array((n_wide, message, panel), BF1...  1.33 us
    pallas_call x1, Pallas kernels, shards(): pl.pallas_call(functools.partial(finish_kernel, total, panel), out_shape=...  0.93 us
    pallas_call x1, Pallas kernels, shards(): pl.pallas_call(functools.partial(gram_kernel, cells, panel), out_shape=(a...  0.91 us
  transfers between devices with their start and end apart: 2, of which 2 were waited for; matrix products, arithmetic and copies ran while one was open for 0% of the time, Pallas kernels for 0%

profile of v2, /device:TPU:0, one launch (start us, length us, event | category | flops | bytes accessed | tf_op | source)
XLA Modules:
  0.0 40.9 jit_solution(446814551486048804)
XLA Ops:
  0.0 1.3 %prep.1 = bf16[8,208,256]{2,1,0:T(8,128)(2,1)S(1)} custom-call(s32[16]{0:T(128)} %assignment.1, s32[2,16]{1,0:T(2,128)} %pairing.1, f32[32,4096]{1,0:T(8,128)} %x_ref.1), custom_call_target="tpu_custom_call" | custom-call | tf_op jit(solution)/shard_map/prep/pallas_call | solution.py:159
  1.3 29.3 %all_to_all.5.here_ref = bf16[8,208,256]{2,1,0:T(8,128)(2,1)S(1)} all-to-all(bf16[8,208,256]{2,1,0:T(8,128)(2,1)S(1)} %prep.1), channel_id=1, replica_groups=mesh['grp'=4,'wide'=8] {'wide'}, dimensions={0} | all-to-all | bytes 1703936 | tf_op jit(solution)/shard_map/all_to_all | solution.py:172
  30.6 0.0 collective-permute-start
  30.6 2.4 %collective-permute-done.there_ref = bf16[8,208,256]{2,1,0:T(8,128)(2,1)S(1)} collective-permute-done((bf16[8,208,256]{2,1,0:T(8,128)(2,1)S(1)}, bf16[8,208,256]{2,1,0:T(8,128)(2,1)S(1)}, u32[]{:S(2)}, u32[]{:S(2)}) %collective-permute-start) | collective-permute-done | bytes 852000 | tf_op jit(solution)/shard_map/ppermute | solution.py:173
  33.0 0.9 %gram.1 = (f32[256,256]{1,0:T(8,128)S(1)}, bf16[304,256]{1,0:T(8,128)(2,1)S(1)}, f32[16,256]{1,0:T(8,128)S(1)}) custom-call(s32[1]{0:T(128)} %bitcast.place, bf16[8,208,256]{2,1,0:T(8,128)(2,1)S(1)} %all_to_all.5.here_ref, bf16[8,208,256]{2,1,0:T(8,128)(2,1)S(1)} %collective-permute-done.there_ref), custom_call_target="tpu_custom_call" | custom-call | tf_op jit(solution)/shard_map/gram/pallas_call | solution.py:175
  33.9 1.6 %collective-permute-start.1 = (bf16[304,256]{1,0:T(8,128)(2,1)S(1)}, bf16[304,256]{1,0:T(8,128)(2,1)S(1)}, u32[]{:S(2)}, u32[]{:S(2)}) collective-permute-start(bf16[304,256]{1,0:T(8,128)(2,1)S(1)} %get-tuple-element.9), channel_id=1, source_target_pairs={{0,16},{8,24},{16,0},{24,8},{1,17},{9,25},{17,1},{25,9},{2,18},{10... | collective-permute-start | bytes 466952 | tf_op jit(solution)/shard_map/ppermute | solution.py:188
  35.4 4.6 %collective-permute-done.1.far_ref = bf16[304,256]{1,0:T(8,128)(2,1)S(1)} collective-permute-done((bf16[304,256]{1,0:T(8,128)(2,1)S(1)}, bf16[304,256]{1,0:T(8,128)(2,1)S(1)}, u32[]{:S(2)}, u32[]{:S(2)}) %collective-permute-start.1) | collective-permute-done | bytes 155680 | tf_op jit(solution)/shard_map/ppermute | solution.py:188
  40.0 0.9 %finish.1 = f32[2,2,64,256]{3,2,1,0:T(8,128)} custom-call(s32[1]{0:T(128)} %bitcast.place, f32[256,256]{1,0:T(8,128)S(1)} %get-tuple-element.8.near_ref, bf16[304,256]{1,0:T(8,128)(2,1)S(1)} %collective-permute-done.1.far_ref, f32[16,256]{1,0:T(8,128)S(1)} %get-tuple-element.10.stat_ref), custom_call_target="tpu_custom_call" | custom-call | tf_op jit(solution)/shard_map/finish/pallas_call | solution.py:189
Async XLA Ops:
  30.6 2.4 %collective-permute-start = (bf16[8,208,256]{2,1,0:T(8,128)(2,1)S(1)}, bf16[8,208,256]{2,1,0:T(8,128)(2,1)S(1)}, u32[]{:S(2)}, u32[]{:S(2)}) collective-permute-start(bf16[8,208,256]{2,1,0:T(8,128)(2,1)S(1)} %all_to_all.5.here_ref), channel_id=1, source_target_pairs={{0,8},{8,0},{16,24},{24,16},{1,9},{9,1},{17,25},{25,17},{2,10},{10... | collective-permute-start | bytes 2555912 | tf_op jit(solution)/shard_map/ppermute | solution.py:173
  33.9 6.1 %collective-permute-start.1 = (bf16[304,256]{1,0:T(8,128)(2,1)S(1)}, bf16[304,256]{1,0:T(8,128)(2,1)S(1)}, u32[]{:S(2)}, u32[]{:S(2)}) collective-permute-start(bf16[304,256]{1,0:T(8,128)(2,1)S(1)} %get-tuple-element.9), channel_id=1, source_target_pairs={{0,16},{8,24},{16,0},{24,8},{1,17},{9,25},{17,1},{25,9},{2,18},{10... | collective-permute-start | bytes 466952 | tf_op jit(solution)/shard_map/ppermute | solution.py:188
